TPU v7x, 256 devices: a whole 4x4x8 slice. The times are simulated.
256 devices in a mesh: tm: 16 (over y_lo, z), orb: 16 (over y_hi, x, core).
Axes of the slice: x: 4, y: 4 (y_hi: 2, y_lo: 2; y = y_hi * 2 + y_lo), z: 8, core: 2. Of those that a mesh axis runs over, the one named last changes fastest.
Arguments:
- self_energy: float32 [16, 2, 8, 1024, 2048], P('tm', None, None, 'orb'), may hold values from -0.0625 to 0.0625
- history: float32 [16, 2, 1024, 1024], P('tm', None, 'orb'), may hold values from -8 to 8
- memory: int32 [1], replicated, may hold values from 3 to 8
- startup_cut: int32 [16], P('tm'), may hold values from 0 to 2048
- weight_index: int32 [16, 8], P('tm'), may hold values from 0 to 15
- weight_table: float32 [16], replicated, may hold values from 0.3 to 3
Outputs:
- collision: float32 [16, 2048, 1024], P('tm', 'orb')
All inputs are finite; a program needn't handle non-finite values.
Results may differ from a plain program's by a relative error of at most 0.0003.
Values sent between devices are 32-bit elements; how exact they have to be, the bound alone decides.
A program may use at most 128 MiB of HBM per device.

v0:
```python
import jax
import jax.numpy as jnp
from jax import lax
from jax.sharding import PartitionSpec as P


def shifted(value, axis, by):
    devices = lax.axis_size(axis)
    pairs = [(i, i + by) for i in range(devices) if 0 <= i + by < devices]
    return lax.ppermute(value, axis, pairs)


def local(self_energy, history, memory, startup_cut, weight_index, weight_table):
    current = history[0]
    lag_count = self_energy.shape[2]
    row_total = self_energy.shape[4]
    table_size = weight_table.shape[0]
    pieces = [current]
    for lag_index in range(1, lag_count):
        current = shifted(current, "tm", 1)
        pieces.append(current)
    lagged = jnp.stack(pieces, axis=1)
    lag_ids = jnp.arange(lag_count, dtype=jnp.int32)[:, None]
    row_ids = jnp.arange(row_total, dtype=jnp.int32)[None, :]
    table_ids = jnp.arange(table_size, dtype=jnp.int32)[None, :]
    weights = jnp.sum(
        jnp.where(weight_index[0][:, None] == table_ids, weight_table[None, :], jnp.float32(0.0)),
        axis=1,
    )
    last_lag = memory[0] - 1
    kept_mask = (lag_ids < last_lag) | (lag_ids == last_lag) & (row_ids >= startup_cut[0])
    coef = jnp.where(kept_mask, weights[:, None], jnp.float32(0.0))
    signs = jnp.array([1.0, -1.0], jnp.float32)[:, None, None, None]
    scaled = self_energy[0] * coef[None, :, None, :] * signs
    partial_sums = lax.dot_general(
        scaled,
        lagged,
        (((0, 1, 2), (0, 1, 2)), ((), ())),
        precision=lax.Precision.HIGHEST,
        preferred_element_type=jnp.float32,
    )
    owned = lax.psum_scatter(partial_sums, "orb", scatter_dimension=0, tiled=True)
    return owned[None]


def solution(mesh):
    in_specs = (
        P("tm", None, None, "orb", None),
        P("tm", None, "orb", None),
        P(),
        P("tm"),
        P("tm", None),
        P(),
    )
    out_specs = P("tm", "orb", None)
    return jax.shard_map(local, mesh=mesh, in_specs=in_specs, out_specs=out_specs, check_vma=False)
```

profile of v0, /device:TPU:8, one launch (start us, length us, event | category | flops | bytes accessed | tf_op | source)
XLA Modules:
  0.0 258.6 jit_solution(15418621748415244635)
XLA Ops:
  6.5 0.0 reduce-scatter.2.cloned.1.call-start
  6.5 3.8 %collective-permute-start = (f32[2,64,1024]{2,1,0:T(8,128)}, f32[2,64,1024]{2,1,0:T(8,128)S(1)}, u32[]{:S(2)}, u32[]{:S(2)}) collective-permute-start(f32[2,64,1024]{2,1,0:T(8,128)} %bitcast.46), channel_id=1, source_target_pairs={{0,16},{16,32},{32,48},{48,64},{64,80},{80,96},{96,112},{112,128},... | collective-permute-start | bytes 1572872 | tf_op jit(solution)/shard_map/ppermute | solution.py:10
  10.4 15.9 %collective-permute-done = f32[2,64,1024]{2,1,0:T(8,128)S(1)} collective-permute-done((f32[2,64,1024]{2,1,0:T(8,128)}, f32[2,64,1024]{2,1,0:T(8,128)S(1)}, u32[]{:S(2)}, u32[]{:S(2)}) %collective-permute-start) | collective-permute-done | bytes 524320 | tf_op jit(solution)/shard_map/ppermute | solution.py:10
  26.3 1.9 collective-permute-start.1
  28.2 15.2 %collective-permute-done.1 = f32[2,64,1024]{2,1,0:T(8,128)S(1)} collective-permute-done((f32[2,64,1024]{2,1,0:T(8,128)S(1)}, f32[2,64,1024]{2,1,0:T(8,128)S(1)}, u32[]{:S(2)}, u32[]{:S(2)}) %collective-permute-start.1) | collective-permute-done | bytes 524320 | tf_op jit(solution)/shard_map/ppermute | solution.py:10
  43.4 1.9 collective-permute-start.2
  45.3 14.3 %collective-permute-done.2 = f32[2,64,1024]{2,1,0:T(8,128)S(1)} collective-permute-done((f32[2,64,1024]{2,1,0:T(8,128)S(1)}, f32[2,64,1024]{2,1,0:T(8,128)S(1)}, u32[]{:S(2)}, u32[]{:S(2)}) %collective-permute-start.2) | collective-permute-done | bytes 524320 | tf_op jit(solution)/shard_map/ppermute | solution.py:10
  59.6 1.9 collective-permute-start.3
  62.8 0.9 select_reduce_fusion
  63.7 0.0 copy-start
  63.7 0.0 copy-start.1
  63.7 1.2 bitcast_dynamic-update-slice_fusion.7
  64.9 10.0 %collective-permute-done.3 = f32[2,64,1024]{2,1,0:T(8,128)S(1)} collective-permute-done((f32[2,64,1024]{2,1,0:T(8,128)S(1)}, f32[2,64,1024]{2,1,0:T(8,128)S(1)}, u32[]{:S(2)}, u32[]{:S(2)}) %collective-permute-start.3) | collective-permute-done | bytes 524320 | tf_op jit(solution)/shard_map/ppermute | solution.py:10
  75.0 1.9 collective-permute-start.4
  76.9 0.1 or_select_fusion
  77.0 12.5 %collective-permute-done.4 = f32[2,64,1024]{2,1,0:T(8,128)S(1)} collective-permute-done((f32[2,64,1024]{2,1,0:T(8,128)S(1)}, f32[2,64,1024]{2,1,0:T(8,128)S(1)}, u32[]{:S(2)}, u32[]{:S(2)}) %collective-permute-start.4) | collective-permute-done | bytes 524320 | tf_op jit(solution)/shard_map/ppermute | solution.py:10
  89.5 1.9 collective-permute-start.5
  91.5 11.6 %collective-permute-done.5 = f32[2,64,1024]{2,1,0:T(8,128)S(1)} collective-permute-done((f32[2,64,1024]{2,1,0:T(8,128)S(1)}, f32[2,64,1024]{2,1,0:T(8,128)S(1)}, u32[]{:S(2)}, u32[]{:S(2)}) %collective-permute-start.5) | collective-permute-done | bytes 524320 | tf_op jit(solution)/shard_map/ppermute | solution.py:10
  103.1 1.9 collective-permute-start.6
  105.2 11.1 %collective-permute-done.6 = f32[2,64,1024]{2,1,0:T(8,128)S(1)} collective-permute-done((f32[2,64,1024]{2,1,0:T(8,128)S(1)}, f32[2,64,1024]{2,1,0:T(8,128)S(1)}, u32[]{:S(2)}, u32[]{:S(2)}) %collective-permute-start.6) | collective-permute-done | bytes 524320 | tf_op jit(solution)/shard_map/ppermute | solution.py:10
  116.4 0.0 copy-done
  116.4 0.0 copy-done.1
  116.4 29.6 %fusion.3 = f32[2048,1024]{1,0:T(8,128)} fusion(f32[2,8,64,1024]{3,2,1,0:T(8,128)S(1)} %bitcast_dynamic-update-slice_fusion.6, f32[1,2,8,64,2048]{4,3,2,1,0:T(8,128)S(1)} %copy-done, f32[2]{0:T(128)S(1)} %copy-done.1, f32[8,2048]{1,0:T(8,128)S(1)} %or_select_fusion), kind=kOutput, calls=%fused_computation.3 | convolution fusion | flops 25773998080 | bytes 21037064 | tf_op jit(solution)/shard_map/dot_general | solution.py:35
  146.0 0.0 reduce-scatter.2.cloned.1.call-update
  146.0 105.7 %reduce-scatter.2.cloned.1.call-done = f32[128,1024]{1,0:T(8,128)} async-done(((f32[2048,1024]{1,0:T(8,128)}), f32[128,1024]{1,0:T(8,128)}) %reduce-scatter.2.cloned.1.call-update) | async-done | bytes 524304 | tf_op jit(solution)/shard_map/reduce_scatter | solution.py:42
  (9 shorter events, 0.3 us)
Async XLA Ops:
  6.5 245.2 %reduce-scatter.2.cloned.1.call-start = ((), (), s32[]{:S(2)}) async-start(), calls=%async_computation.1 | async-start | bytes 8912896 | tf_op jit(solution)/shard_map/reduce_scatter | solution.py:42
  6.5 19.8 %collective-permute-start = (f32[2,64,1024]{2,1,0:T(8,128)}, f32[2,64,1024]{2,1,0:T(8,128)S(1)}, u32[]{:S(2)}, u32[]{:S(2)}) collective-permute-start(f32[2,64,1024]{2,1,0:T(8,128)} %bitcast.46), channel_id=1, source_target_pairs={{0,16},{16,32},{32,48},{48,64},{64,80},{80,96},{96,112},{112,128},... | collective-permute-start | bytes 1572872 | tf_op jit(solution)/shard_map/ppermute | solution.py:10
  26.3 17.1 %collective-permute-start.1 = (f32[2,64,1024]{2,1,0:T(8,128)S(1)}, f32[2,64,1024]{2,1,0:T(8,128)S(1)}, u32[]{:S(2)}, u32[]{:S(2)}) collective-permute-start(f32[2,64,1024]{2,1,0:T(8,128)S(1)} %collective-permute-done), channel_id=1, source_target_pairs={{0,16},{16,32},{32,48},{48,64},{64,80},{80,96},{96,112},{112,128},... | collective-permute-start | bytes 1572872 | tf_op jit(solution)/shard_map/ppermute | solution.py:10
  43.4 16.2 %collective-permute-start.2 = (f32[2,64,1024]{2,1,0:T(8,128)S(1)}, f32[2,64,1024]{2,1,0:T(8,128)S(1)}, u32[]{:S(2)}, u32[]{:S(2)}) collective-permute-start(f32[2,64,1024]{2,1,0:T(8,128)S(1)} %collective-permute-done.1), channel_id=1, source_target_pairs={{0,16},{16,32},{32,48},{48,64},{64,80},{80,96},{96,112},{112,128},... | collective-permute-start | bytes 1572872 | tf_op jit(solution)/shard_map/ppermute | solution.py:10
  59.6 15.4 %collective-permute-start.3 = (f32[2,64,1024]{2,1,0:T(8,128)S(1)}, f32[2,64,1024]{2,1,0:T(8,128)S(1)}, u32[]{:S(2)}, u32[]{:S(2)}) collective-permute-start(f32[2,64,1024]{2,1,0:T(8,128)S(1)} %collective-permute-done.2), channel_id=1, source_target_pairs={{0,16},{16,32},{32,48},{48,64},{64,80},{80,96},{96,112},{112,128},... | collective-permute-start | bytes 1572872 | tf_op jit(solution)/shard_map/ppermute | solution.py:10
  63.7 52.7 %copy-start = (f32[1,2,8,64,2048]{4,3,2,1,0:T(8,128)S(1)}, f32[1,2,8,64,2048]{4,3,2,1,0:T(8,128)}, u32[]{:S(2)}) copy-start(f32[1,2,8,64,2048]{4,3,2,1,0:T(8,128)} %param.7) | copy-start | bytes 25165828
  63.7 52.7 %copy-start.1 = (f32[2]{0:T(128)S(1)}, f32[2]{0:T(128)}, u32[]{:S(2)}) copy-start(f32[2]{0:T(128)} %constant.8.clone) | copy-start | bytes 28
  75.0 14.5 %collective-permute-start.4 = (f32[2,64,1024]{2,1,0:T(8,128)S(1)}, f32[2,64,1024]{2,1,0:T(8,128)S(1)}, u32[]{:S(2)}, u32[]{:S(2)}) collective-permute-start(f32[2,64,1024]{2,1,0:T(8,128)S(1)} %collective-permute-done.3), channel_id=1, source_target_pairs={{0,16},{16,32},{32,48},{48,64},{64,80},{80,96},{96,112},{112,128},... | collective-permute-start | bytes 1572872 | tf_op jit(solution)/shard_map/ppermute | solution.py:10
  89.5 13.7 %collective-permute-start.5 = (f32[2,64,1024]{2,1,0:T(8,128)S(1)}, f32[2,64,1024]{2,1,0:T(8,128)S(1)}, u32[]{:S(2)}, u32[]{:S(2)}) collective-permute-start(f32[2,64,1024]{2,1,0:T(8,128)S(1)} %collective-permute-done.4), channel_id=1, source_target_pairs={{0,16},{16,32},{32,48},{48,64},{64,80},{80,96},{96,112},{112,128},... | collective-permute-start | bytes 1572872 | tf_op jit(solution)/shard_map/ppermute | solution.py:10
  103.1 13.2 %collective-permute-start.6 = (f32[2,64,1024]{2,1,0:T(8,128)S(1)}, f32[2,64,1024]{2,1,0:T(8,128)S(1)}, u32[]{:S(2)}, u32[]{:S(2)}) collective-permute-start(f32[2,64,1024]{2,1,0:T(8,128)S(1)} %collective-permute-done.5), channel_id=1, source_target_pairs={{0,16},{16,32},{32,48},{48,64},{64,80},{80,96},{96,112},{112,128},... | collective-permute-start | bytes 1572872 | tf_op jit(solution)/shard_map/ppermute | solution.py:10
Sparse Core Ops, SparseCore 0:
  146.1 105.5 reduce-scatter.1
where the time goes:
time: 260 us; the launch traced here: 259 us
  waiting for transfers between devices  196 us (75%)
  matrix products  29.6 us (11%)
  starting transfers between devices  15.3 us (6%)
  between operations  14.8 us (6%)
    reduce_scatter x1, waiting for transfers between devices, local(): lax.psum_scatter(partial_sums, 'orb', scatter_dimension=0, tiled=True)  106 us
    ppermute x7, waiting for transfers between devices, shifted(): return lax.ppermute(value, axis, pairs)  90.7 us
    dot_general x1, matrix products, local(): lax.dot_general(scaled, lagged, (((0, 1, 2), (0, 1, 2)), ((), ())), preci...  29.6 us
    ppermute x7, starting transfers between devices, shifted(): return lax.ppermute(value, axis, pairs)  15.3 us
  transfers between devices with their start and end apart: 8, of which 8 were waited for; matrix products, arithmetic and copies ran while one was open for 1% of the time, Pallas kernels for 0%

commit v1 on v0

v1 whole, which is shorter than its diff:
```python
import functools

import jax
import jax.numpy as jnp
from jax import lax
from jax.experimental import pallas as pl
from jax.experimental.pallas import tpu as pltpu
from jax.sharding import PartitionSpec as P

F32 = jnp.float32
BF16 = jnp.bfloat16
MESH = pl.DeviceIdType.MESH
NT = 16
LAGS = 8
CH = 8
W = 128
ORDER = (2, 1, 3, 0)


def halves(value):
    high = value.astype(BF16)
    return high, (value - high.astype(F32)).astype(BF16)


def kernel(
    mem_ref, cut_ref, index_ref, table_ref, hist_ref, se_ref, out_ref,
    stage, rhs, own_hist, gat, gx, own, oth, core_in, a_in, b_in, c_in, y_in,
    se_sem, g_send, g_recv, k_send, k_recv, a_send, a_recv, b_send, b_recv, c_send, c_recv, y_send, y_recv,
):
    t = lax.axis_index("tm")
    o = lax.axis_index("orb")
    yh, x, core = o // 8, (o // 2) % 4, o % 2

    def orb_of(yh_, x_, core_):
        return yh_ * 8 + x_ * 2 + core_

    up, down = t + 1, t - 1
    partner = (t, orb_of(yh, x, 1 - core))
    right = (t, orb_of(yh, (x + 1) % 4, core))
    left = (t, orb_of(yh, (x + 3) % 4, core))
    across = (t, orb_of(1 - yh, x, core))

    for lag in range(LAGS):
        pltpu.make_async_copy(se_ref.at[0, :, lag], stage.at[lag], se_sem.at[lag]).start()

    barrier = pltpu.get_barrier_semaphore()
    greet = [
        (t <= 14, t + 1), (t >= 1, t - 1), (t <= 8, t + 7), (t >= 7, t - 7),
        (t == 9, 15), (t == 10, 15), (t == 15, 9), (t == 15, 10),
    ]
    count = 4
    for there, who in greet:
        count = count + there.astype(jnp.int32)

        @pl.when(there)
        def _():
            pl.semaphore_signal(barrier, inc=1, device_id=(who, o), device_id_type=MESH)

    for who in (partner, right, left, across):
        pl.semaphore_signal(barrier, inc=1, device_id=who, device_id_type=MESH)

    for c in range(CH):
        own_hist[c] = hist_ref[:, c * W:(c + 1) * W].T
    for lag in range(1, LAGS):

        @pl.when(t < lag)
        def _():
            gat[lag] = jnp.zeros((CH, W, W), F32)

    pl.semaphore_wait(barrier, count)

    def remote(src, dst, send, recv, who):
        return pltpu.make_async_remote_copy(
            src_ref=src, dst_ref=dst, send_sem=send, recv_sem=recv, device_id=who, device_id_type=MESH
        )

    def send_own_up(c):
        return remote(own_hist.at[c], gat.at[1, c], g_send.at[1, c], g_recv.at[1, c], (up, o))

    def send_own_far(c):
        lag = 7 - jnp.maximum(t - 8, 0)
        return remote(own_hist.at[c], gat.at[lag, c], g_send.at[7, c], g_recv.at[lag, c], (jnp.minimum(t + 7, 15), o))

    def relay(lag, c):
        if lag <= 4:
            return remote(gat.at[lag - 1, c], gat.at[lag, c], g_send.at[lag, c], g_recv.at[lag, c], (up, o))
        return remote(gat.at[lag + 1, c], gat.at[lag, c], g_send.at[lag, c], g_recv.at[lag, c], (down, o))

    def relays(lag):
        if lag <= 4:
            return (t <= 14) & (t + 1 >= lag)
        return t - 1 >= lag

    def arrived(lag, c):
        remote(gat.at[lag, c], gat.at[lag, c], g_send.at[lag, c], g_recv.at[lag, c], partner).wait_recv()

    def inside(c):
        return (c >= 0) & (c < CH)

    def take_and_relay(lag, nxt, c):
        @pl.when(inside(c) & (t >= lag))
        def _():
            arrived(lag, c)

        if nxt is not None:

            @pl.when(inside(c) & relays(nxt))
            def _():
                relay(nxt, c).start()

    def to_partner(d, c):
        return remote(oth.at[c, d], core_in.at[c, d], k_send.at[d, c], k_recv.at[d, c], partner)

    def add_partner(d, c):
        to_partner(d, c).wait_recv()
        own[c, d] = own[c, d] + core_in[c, d]

    def a_copy(way, c):
        return remote(own.at[c, 2, way], a_in.at[way, c], a_send.at[way, c], a_recv.at[way, c], (right, left)[way])

    def b_copy(way, c):
        d = (1, 3)[way]
        return remote(own.at[c, d, 1 - way], b_in.at[way, c], b_send.at[way, c], b_recv.at[way, c], (right, left)[way])

    def c_copy(way, c):
        d = (1, 3)[way]
        return remote(own.at[c, d, way], c_in.at[way, c], c_send.at[way, c], c_recv.at[way, c], (right, left)[way])

    def y_copy(c):
        return remote(own.at[c, 0, 1 - yh], y_in.at[c], y_send.at[c], y_recv.at[c], across)

    def prepare(lag):
        pltpu.make_async_copy(se_ref.at[0, :, lag], stage.at[lag], se_sem.at[lag]).wait()
        weight = table_ref[index_ref[0, lag]]
        last = mem_ref[0] - 1
        base = pl.multiple_of(lag * W, W)
        low_base = pl.multiple_of(LAGS * W + lag * W, W)
        for d in range(4):
            for side in range(2):
                for yh_ in range(2):
                    col = pl.multiple_of(yh_ * 1024 + ((x + d) % 4) * 256 + (core if side == 0 else 1 - core) * W, W)
                    rows = col + lax.broadcasted_iota(jnp.int32, (64, W), 1)
                    kept = (lag < last) | ((lag == last) & (rows >= cut_ref[0]))
                    coef = jnp.where(kept, weight, F32(0.0))
                    place = pl.ds((d * 4 + side * 2 + yh_) * W, W)
                    value = jnp.concatenate(
                        [stage[lag, 0, :, pl.ds(col, W)] * coef, -(stage[lag, 1, :, pl.ds(col, W)] * coef)], axis=0
                    )
                    high, low = halves(value)
                    rhs[pl.ds(base, W), place] = high
                    rhs[pl.ds(low_base, W), place] = low

    def load_left(c):
        for lag in range(LAGS):
            high, low = halves(own_hist[c] if lag == 0 else gat[lag, c])
            gx[:W, lag * W:(lag + 1) * W] = high
            gx[W:, lag * W:(lag + 1) * W] = low

    def multiply(d, c):
        cols = pl.ds(d * 512, 512)
        both = jnp.dot(gx[...], rhs[:LAGS * W, cols], preferred_element_type=F32)
        more = jnp.dot(gx[:W], rhs[LAGS * W:, cols], preferred_element_type=F32)
        total = both[:W] + both[W:] + more
        for yh_ in range(2):
            own[c, d, yh_] = total[:, yh_ * W:(yh_ + 1) * W]
            oth[c, d, yh_] = total[:, (2 + yh_) * W:(3 + yh_) * W]
        to_partner(d, c).start()

    def step(s, carry):
        for slot in range(4):
            if slot == 0:

                @pl.when(inside(s + 3) & (t <= 14))
                def _():
                    send_own_up(s + 3).start()

                @pl.when(inside(s + 2) & (t <= 10))
                def _():
                    send_own_far(s + 2).start()

                @pl.when(inside(s - 1))
                def _():
                    c = s - 1
                    add_partner(2, c)
                    a_copy(0, c).start()
                    a_copy(1, c).start()
                    add_partner(1, c)
                    b_copy(0, c).start()
                    add_partner(3, c)
                    b_copy(1, c).start()

                @pl.when(inside(s - 3))
                def _():
                    c = s - 3
                    y_copy(c).wait_recv()
                    total = own[c, 0, yh] + y_in[c]
                    out_ref[:, pl.ds(pl.multiple_of(c * W, W), W)] = total.T

                take_and_relay(4, None, s)
                take_and_relay(5, None, s)

                @pl.when(inside(s))
                def _():
                    load_left(s)

            if slot == 1:
                take_and_relay(3, 4, s + 1)

                @pl.when(inside(s - 1))
                def _():
                    add_partner(0, s - 1)

                @pl.when(inside(s - 2))
                def _():
                    c = s - 2
                    for way in range(2):
                        b_copy(way, c).wait_recv()
                        c_copy(way, c).wait_recv()
                    own[c, 0, 0] = own[c, 0, 0] + (c_in[0, c] + b_in[1, c])
                    own[c, 0, 1] = own[c, 0, 1] + (b_in[0, c] + c_in[1, c])
                    y_copy(c).start()

            if slot == 2:
                take_and_relay(2, 3, s + 2)
                take_and_relay(6, 5, s + 1)

                @pl.when(inside(s - 1))
                def _():
                    c = s - 1
                    for way in range(2):
                        d = (1, 3)[way]
                        a_copy(way, c).wait_recv()
                        own[c, d, way] = own[c, d, way] + a_in[way, c]
                        c_copy(way, c).start()

            if slot == 3:
                take_and_relay(1, 2, s + 3)
                take_and_relay(7, 6, s + 2)

            @pl.when(inside(s))
            def _():
                multiply(ORDER[slot], s)

            lag = (s + 3) * 4 + slot

            @pl.when(lag < LAGS)
            def _():
                prepare(lag)

        return carry

    lax.fori_loop(-3, CH + 3, step, 0)

    def drain(c, carry):
        @pl.when(t <= 14)
        def _():
            send_own_up(c).wait_send()

        @pl.when(t <= 10)
        def _():
            send_own_far(c).wait_send()

        for lag in (2, 3, 4, 5, 6):

            @pl.when(relays(lag))
            def _():
                relay(lag, c).wait_send()

        for d in range(4):
            to_partner(d, c).wait_send()
        for way in range(2):
            a_copy(way, c).wait_send()
            b_copy(way, c).wait_send()
            c_copy(way, c).wait_send()
        y_copy(c).wait_send()
        return carry

    lax.fori_loop(0, CH, drain, 0)


def local(self_energy, history, memory, startup_cut, weight_index, weight_table):
    smem = pl.BlockSpec(memory_space=pltpu.SMEM)
    vmem = pl.BlockSpec(memory_space=pltpu.VMEM)
    dma = pltpu.SemaphoreType.DMA
    piece = (W, W)
    out = pl.pallas_call(
        kernel,
        out_shape=jax.ShapeDtypeStruct((W, CH * W), F32),
        in_specs=[smem, smem, smem, smem, vmem, pl.BlockSpec(memory_space=pl.ANY)],
        out_specs=vmem,
        scratch_shapes=[
            pltpu.VMEM((LAGS, 2, 64, 2048), F32),
            pltpu.VMEM((2 * LAGS * W, 2048), BF16),
            pltpu.VMEM((CH, *piece), F32),
            pltpu.VMEM((LAGS, CH, *piece), F32),
            pltpu.VMEM((2 * W, LAGS * W), BF16),
            pltpu.VMEM((CH, 4, 2, *piece), F32),
            pltpu.VMEM((CH, 4, 2, *piece), F32),
            pltpu.VMEM((CH, 4, 2, *piece), F32),
            pltpu.VMEM((2, CH, *piece), F32),
            pltpu.VMEM((2, CH, *piece), F32),
            pltpu.VMEM((2, CH, *piece), F32),
            pltpu.VMEM((CH, *piece), F32),
            dma((LAGS,)),
            dma((LAGS, CH)), dma((LAGS, CH)),
            dma((4, CH)), dma((4, CH)),
            dma((2, CH)), dma((2, CH)),
            dma((2, CH)), dma((2, CH)),
            dma((2, CH)), dma((2, CH)),
            dma((CH,)), dma((CH,)),
        ],
        compiler_params=pltpu.CompilerParams(
            collective_id=0, has_side_effects=True, vmem_limit_bytes=60 * 1024 * 1024
        ),
        name="collision",
    )(memory, startup_cut, weight_index, weight_table, history.reshape(2 * 64, 1024), self_energy)
    return out[None]


def solution(mesh):
    in_specs = (
        P("tm", None, None, "orb", None),
        P("tm", None, "orb", None),
        P(),
        P("tm"),
        P("tm", None),
        P(),
    )
    out_specs = P("tm", "orb", None)
    return jax.shard_map(local, mesh=mesh, in_specs=in_specs, out_specs=out_specs, check_vma=False)
```

time: 260 us -> 106 us (0.41)
  the two profiles are of different devices: /device:TPU:8 before, /device:TPU:4 now
where the time goes in v1:
time: 106 us; the launch traced here: 105 us
  Pallas kernels  102 us (96%)
  local copies, waits for them, and re-layouts  1.89 us (2%)
  between operations  1.3 us (1%)
    pallas_call x1, Pallas kernels, local(): pl.pallas_call(kernel, out_shape=jax.ShapeDtypeStruct((W, CH * W), F32),...  102 us

profile of v1, /device:TPU:4, one launch (start us, length us, event | category | flops | bytes accessed | tf_op | source)
XLA Modules:
  0.0 105.5 jit_solution(5952611385173554121)
XLA Ops:
  1.3 102.3 %collision.1 = f32[128,1024]{1,0:T(8,128)} custom-call(s32[1]{0:T(128)S(6)} %copy.8.mem_ref, s32[1]{0:T(128)S(6)} %copy.9.cut_ref, s32[1,8]{1,0:T(1,128)} %index_ref.1, f32[16]{0:T(128)} %table_ref.1, f32[128,1024]{1,0:T(8,128)} %bitcast.3, f32[1,2,8,64,2048]{4,3,2,1,0:T(8,128)} %se_ref.1), custom_call_target="tpu_custom_call" | custom-call | tf_op jit(solution)/shard_map/collision/pallas_call | solution.py:286
  103.6 1.9 %copy.10 = f32[1,128,1024]{2,1,0:T(8,128)} copy(f32[1,128,1024]{2,1,0:T(8,128)} %bitcast.2) | data formatting | bytes 1048576

commit v2 on v1

--- a/solution.py
+++ b/solution.py
@@ -24,8 +24,8 @@
 
 def kernel(
     mem_ref, cut_ref, index_ref, table_ref, hist_ref, se_ref, out_ref,
-    stage, rhs, own_hist, gat, gx, own, oth, core_in, a_in, b_in, c_in, y_in,
-    se_sem, g_send, g_recv, k_send, k_recv, a_send, a_recv, b_send, b_recv, c_send, c_recv, y_send, y_recv,
+    stage, rhs, own_hist, gat, via, gx, own, oth, core_in, a_in, b_in, c_in, y_in,
+    se_sem, g_send, g_recv, v_recv, k_send, k_recv, a_send, a_recv, b_send, b_recv, c_send, c_recv, y_send, y_recv,
 ):
     t = lax.axis_index("tm")
     o = lax.axis_index("orb")
@@ -45,8 +45,8 @@
 
     barrier = pltpu.get_barrier_semaphore()
     greet = [
-        (t <= 14, t + 1), (t >= 1, t - 1), (t <= 8, t + 7), (t >= 7, t - 7),
-        (t == 9, 15), (t == 10, 15), (t == 15, 9), (t == 15, 10),
+        (t <= 14, t + 1), (t >= 1, t - 1), (t <= 6, t + 8), ((t >= 8) & (t <= 14), t - 8),
+        (t == 0, 7), (t == 7, 0), ((t >= 8) & (t <= 10), 15), (t == 15, 8), (t == 15, 9), (t == 15, 10),
     ]
     count = 4
     for there, who in greet:
@@ -79,7 +79,26 @@
 
     def send_own_far(c):
         lag = 7 - jnp.maximum(t - 8, 0)
-        return remote(own_hist.at[c], gat.at[lag, c], g_send.at[7, c], g_recv.at[lag, c], (jnp.minimum(t + 7, 15), o))
+        return remote(
+            own_hist.at[c], gat.at[lag, c], g_send.at[7, c], g_recv.at[lag, c], (jnp.where(t == 0, 7, 15), o)
+        )
+
+    far = (t == 0) | ((t >= 8) & (t <= 10))
+
+    def send_own_via(c):
+        return remote(own_hist.at[c], via.at[0, c], g_send.at[7, c], v_recv.at[0, c], (down, o))
+
+    def pass_own_via(c):
+        return remote(via.at[0, c], gat.at[7, c], g_send.at[0, c], g_recv.at[7, c], (t + 8, o))
+
+    by_via = (t >= 1) & (t <= 7)
+    passes = t <= 6
+
+    def relay_via(lag, c):
+        return remote(gat.at[lag - 1, c], via.at[lag - 2, c], g_send.at[lag, c], v_recv.at[lag - 2, c], (0, o))
+
+    def pass_relay_via(lag, c):
+        return remote(via.at[lag - 2, c], gat.at[lag, c], g_send.at[lag, c], g_recv.at[lag, c], (8, o))
 
     def relay(lag, c):
         if lag <= 4:
@@ -87,9 +106,9 @@
         return remote(gat.at[lag + 1, c], gat.at[lag, c], g_send.at[lag, c], g_recv.at[lag, c], (down, o))
 
     def relays(lag):
-        if lag <= 4:
-            return (t <= 14) & (t + 1 >= lag)
-        return t - 1 >= lag
+        if lag >= 5:
+            return t - 1 >= lag
+        return (t <= 14) & (t + 1 >= lag) & ((t != 7) | (lag <= 2))
 
     def arrived(lag, c):
         remote(gat.at[lag, c], gat.at[lag, c], g_send.at[lag, c], g_recv.at[lag, c], partner).wait_recv()
@@ -107,6 +126,12 @@
             @pl.when(inside(c) & relays(nxt))
             def _():
                 relay(nxt, c).start()
+
+        if nxt in (3, 4):
+
+            @pl.when(inside(c) & (t == 7))
+            def _():
+                relay_via(nxt, c).start()
 
     def to_partner(d, c):
         return remote(oth.at[c, d], core_in.at[c, d], k_send.at[d, c], k_recv.at[d, c], partner)
@@ -174,9 +199,13 @@
                 def _():
                     send_own_up(s + 3).start()
 
-                @pl.when(inside(s + 2) & (t <= 10))
-                def _():
-                    send_own_far(s + 2).start()
+                @pl.when(inside(s + 3) & far)
+                def _():
+                    send_own_far(s + 3).start()
+
+                @pl.when(inside(s + 3) & by_via)
+                def _():
+                    send_own_via(s + 3).start()
 
                 @pl.when(inside(s - 1))
                 def _():
@@ -237,6 +266,18 @@
                 take_and_relay(1, 2, s + 3)
                 take_and_relay(7, 6, s + 2)
 
+                @pl.when(inside(s + 3) & passes)
+                def _():
+                    send_own_via(s + 3).wait_recv()
+                    pass_own_via(s + 3).start()
+
+                for lag in (4, 3):
+
+                    @pl.when(inside(s + 5 - lag) & (t == 0))
+                    def _():
+                        relay_via(lag, s + 5 - lag).wait_recv()
+                        pass_relay_via(lag, s + 5 - lag).start()
+
             @pl.when(inside(s))
             def _():
                 multiply(ORDER[slot], s)
@@ -256,9 +297,23 @@
         def _():
             send_own_up(c).wait_send()
 
-        @pl.when(t <= 10)
+        @pl.when(far)
         def _():
             send_own_far(c).wait_send()
+
+        @pl.when(by_via)
+        def _():
+            send_own_via(c).wait_send()
+
+        @pl.when(passes)
+        def _():
+            pass_own_via(c).wait_send()
+
+        for lag in (3, 4):
+
+            @pl.when((t == 0) | (t == 7))
+            def _():
+                relay_via(lag, c).wait_send()
 
         for lag in (2, 3, 4, 5, 6):
 
@@ -293,6 +348,7 @@
             pltpu.VMEM((2 * LAGS * W, 2048), BF16),
             pltpu.VMEM((CH, *piece), F32),
             pltpu.VMEM((LAGS, CH, *piece), F32),
+            pltpu.VMEM((3, CH, *piece), F32),
             pltpu.VMEM((2 * W, LAGS * W), BF16),
             pltpu.VMEM((CH, 4, 2, *piece), F32),
             pltpu.VMEM((CH, 4, 2, *piece), F32),
@@ -302,7 +358,7 @@
             pltpu.VMEM((2, CH, *piece), F32),
             pltpu.VMEM((CH, *piece), F32),
             dma((LAGS,)),
-            dma((LAGS, CH)), dma((LAGS, CH)),
+            dma((LAGS, CH)), dma((LAGS, CH)), dma((3, CH)),
             dma((4, CH)), dma((4, CH)),
             dma((2, CH)), dma((2, CH)),
             dma((2, CH)), dma((2, CH)),

time: 106 us -> 108 us (1.019)
  the two profiles are of different devices: /device:TPU:4 before, /device:TPU:8 now
where the time goes in v2:
time: 108 us
  Pallas kernels  105 us (97%)
  local copies, waits for them, and re-layouts  1.89 us (2%)
  between operations  1.3 us (1%)
    pallas_call x1, Pallas kernels, local(): pl.pallas_call(kernel, out_shape=jax.ShapeDtypeStruct((W, CH * W), F32),...  105 us

profile of v2, /device:TPU:8, one launch (start us, length us, event | category | flops | bytes accessed | tf_op | source)
XLA Modules:
  0.0 108.0 jit_solution(4519322088037951328)
XLA Ops:
  1.3 104.8 %collision.1 = f32[128,1024]{1,0:T(8,128)} custom-call(s32[1]{0:T(128)S(6)} %copy.8.mem_ref, s32[1]{0:T(128)S(6)} %copy.9.cut_ref, s32[1,8]{1,0:T(1,128)} %index_ref.1, f32[16]{0:T(128)} %table_ref.1, f32[128,1024]{1,0:T(8,128)} %bitcast.3, f32[1,2,8,64,2048]{4,3,2,1,0:T(8,128)} %se_ref.1), custom_call_target="tpu_custom_call" | custom-call | tf_op jit(solution)/shard_map/collision/pallas_call | solution.py:341
  106.1 1.9 %copy.10 = f32[1,128,1024]{2,1,0:T(8,128)} copy(f32[1,128,1024]{2,1,0:T(8,128)} %bitcast.2) | data formatting | bytes 1048576

commit v3 on v2

--- a/solution.py
+++ b/solution.py
@@ -15,6 +15,11 @@
 CH = 8
 W = 128
 ORDER = (2, 1, 3, 0)
+AT = {
+    "S1": -24, "D7": -17, "R2": -16, "V": -12, "R6": -11, "R3": -10, "V3": -7, "R4": -5, "R5": -5, "V4": -2,
+    "W": 0, "KA": 3, "KB": 4, "K0": 7, "C": 7, "X": 12, "F": 20,
+}
+PLAN = ("S1", "V", "X", "R5", "R3", "KA", "F", "R6", "C", "KB", "W", "V4", "K0", "R4", "D7", "R2", "V3")
 
 
 def halves(value):
@@ -191,106 +196,127 @@
             oth[c, d, yh_] = total[:, (2 + yh_) * W:(3 + yh_) * W]
         to_partner(d, c).start()
 
+    def run(name, c):
+        def when(cond):
+            return pl.when(inside(c) & cond)
+
+        if name == "S1":
+
+            @when(t <= 14)
+            def _():
+                send_own_up(c).start()
+
+        if name == "D7":
+
+            @when(far)
+            def _():
+                send_own_far(c).start()
+
+            @when(by_via)
+            def _():
+                send_own_via(c).start()
+
+        if name == "V":
+
+            @when(passes)
+            def _():
+                send_own_via(c).wait_recv()
+                pass_own_via(c).start()
+
+        if name in ("V3", "V4"):
+            lag = int(name[1])
+
+            @when(t == 0)
+            def _():
+                relay_via(lag, c).wait_recv()
+                pass_relay_via(lag, c).start()
+
+        if name in ("R2", "R3", "R4"):
+            take_and_relay(int(name[1]) - 1, int(name[1]), c)
+        if name in ("R5", "R6"):
+            take_and_relay(int(name[1]) + 1, int(name[1]), c)
+        if name == "W":
+            take_and_relay(4, None, c)
+            take_and_relay(5, None, c)
+
+            @pl.when(inside(c))
+            def _():
+                load_left(c)
+
+        if name == "KA":
+
+            @pl.when(inside(c))
+            def _():
+                add_partner(2, c)
+                a_copy(0, c).start()
+                a_copy(1, c).start()
+
+        if name == "KB":
+
+            @pl.when(inside(c))
+            def _():
+                add_partner(1, c)
+                b_copy(0, c).start()
+                add_partner(3, c)
+                b_copy(1, c).start()
+
+        if name == "K0":
+
+            @pl.when(inside(c))
+            def _():
+                add_partner(0, c)
+
+        if name == "C":
+
+            @pl.when(inside(c))
+            def _():
+                for way in range(2):
+                    d = (1, 3)[way]
+                    a_copy(way, c).wait_recv()
+                    own[c, d, way] = own[c, d, way] + a_in[way, c]
+                    c_copy(way, c).start()
+
+        if name == "X":
+
+            @pl.when(inside(c))
+            def _():
+                for way in range(2):
+                    b_copy(way, c).wait_recv()
+                    c_copy(way, c).wait_recv()
+                own[c, 0, 0] = own[c, 0, 0] + (c_in[0, c] + b_in[1, c])
+                own[c, 0, 1] = own[c, 0, 1] + (b_in[0, c] + c_in[1, c])
+                y_copy(c).start()
+
+        if name == "F":
+
+            @pl.when(inside(c))
+            def _():
+                y_copy(c).wait_recv()
+                total = own[c, 0, yh] + y_in[c]
+                out_ref[:, pl.ds(pl.multiple_of(c * W, W), W)] = total.T
+
+    first = min(AT.values()) // 4
+    last = CH + max(AT.values()) // 4
+
     def step(s, carry):
         for slot in range(4):
-            if slot == 0:
-
-                @pl.when(inside(s + 3) & (t <= 14))
-                def _():
-                    send_own_up(s + 3).start()
-
-                @pl.when(inside(s + 3) & far)
-                def _():
-                    send_own_far(s + 3).start()
-
-                @pl.when(inside(s + 3) & by_via)
-                def _():
-                    send_own_via(s + 3).start()
-
-                @pl.when(inside(s - 1))
-                def _():
-                    c = s - 1
-                    add_partner(2, c)
-                    a_copy(0, c).start()
-                    a_copy(1, c).start()
-                    add_partner(1, c)
-                    b_copy(0, c).start()
-                    add_partner(3, c)
-                    b_copy(1, c).start()
-
-                @pl.when(inside(s - 3))
-                def _():
-                    c = s - 3
-                    y_copy(c).wait_recv()
-                    total = own[c, 0, yh] + y_in[c]
-                    out_ref[:, pl.ds(pl.multiple_of(c * W, W), W)] = total.T
-
-                take_and_relay(4, None, s)
-                take_and_relay(5, None, s)
-
-                @pl.when(inside(s))
-                def _():
-                    load_left(s)
-
-            if slot == 1:
-                take_and_relay(3, 4, s + 1)
-
-                @pl.when(inside(s - 1))
-                def _():
-                    add_partner(0, s - 1)
-
-                @pl.when(inside(s - 2))
-                def _():
-                    c = s - 2
-                    for way in range(2):
-                        b_copy(way, c).wait_recv()
-                        c_copy(way, c).wait_recv()
-                    own[c, 0, 0] = own[c, 0, 0] + (c_in[0, c] + b_in[1, c])
-                    own[c, 0, 1] = own[c, 0, 1] + (b_in[0, c] + c_in[1, c])
-                    y_copy(c).start()
-
-            if slot == 2:
-                take_and_relay(2, 3, s + 2)
-                take_and_relay(6, 5, s + 1)
-
-                @pl.when(inside(s - 1))
-                def _():
-                    c = s - 1
-                    for way in range(2):
-                        d = (1, 3)[way]
-                        a_copy(way, c).wait_recv()
-                        own[c, d, way] = own[c, d, way] + a_in[way, c]
-                        c_copy(way, c).start()
-
-            if slot == 3:
-                take_and_relay(1, 2, s + 3)
-                take_and_relay(7, 6, s + 2)
-
-                @pl.when(inside(s + 3) & passes)
-                def _():
-                    send_own_via(s + 3).wait_recv()
-                    pass_own_via(s + 3).start()
-
-                for lag in (4, 3):
-
-                    @pl.when(inside(s + 5 - lag) & (t == 0))
-                    def _():
-                        relay_via(lag, s + 5 - lag).wait_recv()
-                        pass_relay_via(lag, s + 5 - lag).start()
+            for name in PLAN:
+                if AT[name] % 4 == slot:
+                    run(name, s - AT[name] // 4)
 
             @pl.when(inside(s))
             def _():
                 multiply(ORDER[slot], s)
 
-            lag = (s + 3) * 4 + slot
-
-            @pl.when(lag < LAGS)
+            lag = (s + 4) * 4 + slot
+
+            @pl.when((lag >= 0) & (lag < LAGS))
             def _():
                 prepare(lag)
 
         return carry
 
-    lax.fori_loop(-3, CH + 3, step, 0)
+    lax.fori_loop(first, last + 1, step, 0)
 
     def drain(c, carry):
         @pl.when(t <= 14)

time: 108 us -> 101 us (0.935)
  Pallas kernels: 105 us -> 97.8 us
    pallas_call x1, Pallas kernels: 105 us -> 97.8 us  [local(): pl.pallas_call(kernel, out_shape=jax.ShapeDtypeStruct((W, CH * W), F32),...]
where the time goes in v3:
time: 101 us
  Pallas kernels  97.8 us (97%)
  local copies, waits for them, and re-layouts  1.89 us (2%)
  between operations  1.3 us (1%)
    pallas_call x1, Pallas kernels, local(): pl.pallas_call(kernel, out_shape=jax.ShapeDtypeStruct((W, CH * W), F32),...  97.8 us

profile of v3, /device:TPU:8, one launch (start us, length us, event | category | flops | bytes accessed | tf_op | source)
XLA Modules:
  0.0 101.0 jit_solution(4505019619214200891)
XLA Ops:
  1.3 97.8 %collision.1 = f32[128,1024]{1,0:T(8,128)} custom-call(s32[1]{0:T(128)S(6)} %copy.8.mem_ref, s32[1]{0:T(128)S(6)} %copy.9.cut_ref, s32[1,8]{1,0:T(1,128)} %index_ref.1, f32[16]{0:T(128)} %table_ref.1, f32[128,1024]{1,0:T(8,128)} %bitcast.3, f32[1,2,8,64,2048]{4,3,2,1,0:T(8,128)} %se_ref.1), custom_call_target="tpu_custom_call" | custom-call | tf_op jit(solution)/shard_map/collision/pallas_call | solution.py:367
  99.1 1.9 %copy.10 = f32[1,128,1024]{2,1,0:T(8,128)} copy(f32[1,128,1024]{2,1,0:T(8,128)} %bitcast.2) | data formatting | bytes 1048576

commit v4 on v3

v4 whole, which is shorter than its diff:
```python
import functools

import jax
import jax.numpy as jnp
from jax import lax
from jax.experimental import pallas as pl
from jax.experimental.pallas import tpu as pltpu
from jax.sharding import PartitionSpec as P

F32 = jnp.float32
BF16 = jnp.bfloat16
MESH = pl.DeviceIdType.MESH
NT = 16
LAGS = 8
CH = 8
W = 128
ORDER = (2, 1, 3, 0)
AT = {
    "S1": -24, "D7": -11, "R2": -16, "R6": -7, "R3": -10, "R4": -5, "R5": -3, "P1": -22,
    "P2": -12, "W": 0, "KA": 3, "KB": 4, "K0": 11, "C": 6, "X": 12, "F": 16,
}
PLAN = ("X", "KA", "D7", "KB", "P1", "S1", "F", "R3", "W", "K0", "C", "R5", "R4", "P2", "R2", "R6")


def halves(value):
    high = value.astype(BF16)
    return high, (value - high.astype(F32)).astype(BF16)


def kernel(
    mem_ref, cut_ref, index_ref, table_ref, hist_ref, se_ref, out_ref,
    stage, rhs, own_hist, gat, via, gx, own, oth, core_in, a_in, bc_in, y_in,
    se_sem, g_send, g_recv, v_recv, k_send, k_recv, a_send, a_recv, b_send, c_send, bc_recv, y_send, y_recv,
):
    t = lax.axis_index("tm")
    o = lax.axis_index("orb")
    yh, x, core = o // 8, (o // 2) % 4, o % 2

    def orb_of(yh_, x_, core_):
        return yh_ * 8 + x_ * 2 + core_

    up, down = t + 1, t - 1
    partner = (t, orb_of(yh, x, 1 - core))
    right = (t, orb_of(yh, (x + 1) % 4, core))
    left = (t, orb_of(yh, (x + 3) % 4, core))
    across = (t, orb_of(1 - yh, x, core))

    for lag in range(LAGS):
        pltpu.make_async_copy(se_ref.at[0, :, lag], stage.at[lag], se_sem.at[lag]).start()

    barrier = pltpu.get_barrier_semaphore()
    greet = [
        (t <= 14, t + 1), (t >= 1, t - 1), (t <= 8, t + 7), (t >= 7, t - 7),
        ((t == 9) | (t == 10), 15), (t == 15, 9), (t == 15, 10),
        ((t == 1) | (t == 2), 7), (t == 7, 1), (t == 7, 2), (t == 7, 15), (t == 15, 7),
    ]
    count = 4
    for there, who in greet:
        count = count + there.astype(jnp.int32)

        @pl.when(there)
        def _():
            pl.semaphore_signal(barrier, inc=1, device_id=(who, o), device_id_type=MESH)

    for who in (partner, right, left, across):
        pl.semaphore_signal(barrier, inc=1, device_id=who, device_id_type=MESH)

    for c in range(CH):
        own_hist[c] = hist_ref[:, c * W:(c + 1) * W].T
    for lag in range(1, LAGS):

        @pl.when(t < lag)
        def _():
            gat[lag] = jnp.zeros((CH, W, W), F32)

    pl.semaphore_wait(barrier, count)

    def remote(src, dst, send, recv, who):
        return pltpu.make_async_remote_copy(
            src_ref=src, dst_ref=dst, send_sem=send, recv_sem=recv, device_id=who, device_id_type=MESH
        )

    def go(make, c):
        @pl.when(c >= 2)
        def _():
            make(c - 2).wait_send()

        make(c).start()

    def history(src, lag, c, kind, who):
        return remote(src, gat.at[lag, c], g_send.at[kind, c % 2], g_recv.at[lag, c], (who, o))

    def send_own_up(c):
        return history(own_hist.at[c], 1, c, 1, up)

    def relay(lag, c):
        if lag <= 4:
            return history(gat.at[lag - 1, c], lag, c, lag, up)
        return history(gat.at[lag + 1, c], lag, c, lag, down)

    def send_own_far(c):
        return history(own_hist.at[c], 7 - jnp.maximum(t - 8, 0), c, 7, jnp.minimum(t + 7, 15))

    def send_own_seven(c):
        return history(own_hist.at[c], 7 - t, c, 6, 7)

    def relay_via(lag, c):
        src = own_hist.at[c] if lag == 1 else gat.at[1, c]
        return remote(src, via.at[lag - 1, c], g_send.at[lag, c % 2], v_recv.at[lag - 1, c], (15, o))

    def pass_via(lag, c):
        return history(via.at[lag - 1, c], lag, c, lag, 8)

    def relays(lag):
        if lag >= 5:
            return (t - 1 >= lag) & (t != 8)
        return (t <= 14) & (t + 1 >= lag) & ((t != 7) | (lag >= 3))

    def arrived(lag, c):
        remote(gat.at[lag, c], gat.at[lag, c], g_send.at[lag, 0], g_recv.at[lag, c], partner).wait_recv()

    def inside(c):
        return (c >= 0) & (c < CH)

    def take_and_relay(lag, nxt, c):
        @pl.when(inside(c) & (t >= lag))
        def _():
            arrived(lag, c)

        if nxt is not None:

            @pl.when(inside(c) & relays(nxt))
            def _():
                go(functools.partial(relay, nxt), c)

        if nxt == 2:

            @pl.when(inside(c) & (t == 7))
            def _():
                go(functools.partial(relay_via, 2), c)

    def to_partner(q, c):
        return remote(oth.at[c, q], core_in.at[c, q], k_send.at[q, c % 2], k_recv.at[(0, 1, 1, 2)[q], c], partner)

    def add_partner(start, size, c):
        part = core_in.at[c, pl.ds(start, size)]
        remote(part, part, k_send.at[start, c % 2], k_recv.at[(0, 1, 1, 2)[start], c], partner).wait_recv()
        own[c, pl.ds(start, size)] = own[c, pl.ds(start, size)] + core_in[c, pl.ds(start, size)]

    def a_copy(way, c):
        return remote(own.at[c, 0, way], a_in.at[c, way], a_send.at[way, c % 2], a_recv.at[c], (right, left)[way])

    def b_copy(way, c):
        return remote(
            own.at[c, 1 + way, 1 - way], bc_in.at[c, way], b_send.at[way, c % 2], bc_recv.at[c], (right, left)[way]
        )

    def c_copy(way, c):
        return remote(
            own.at[c, 1 + way, way], bc_in.at[c, 2 + way], c_send.at[way, c % 2], bc_recv.at[c], (right, left)[way]
        )

    def y_copy(c):
        return remote(own.at[c, 3, 1 - yh], y_in.at[c], y_send.at[c % 2], y_recv.at[c], across)

    def prepare(lag):
        pltpu.make_async_copy(se_ref.at[0, :, lag], stage.at[lag], se_sem.at[lag]).wait()
        weight = table_ref[index_ref[0, lag]]
        last = mem_ref[0] - 1
        base = pl.multiple_of(lag * W, W)
        low_base = pl.multiple_of(LAGS * W + lag * W, W)
        for q, d in enumerate(ORDER):
            for side in range(2):
                for yh_ in range(2):
                    col = pl.multiple_of(yh_ * 1024 + ((x + d) % 4) * 256 + (core if side == 0 else 1 - core) * W, W)
                    rows = col + lax.broadcasted_iota(jnp.int32, (64, W), 1)
                    kept = (lag < last) | ((lag == last) & (rows >= cut_ref[0]))
                    coef = jnp.where(kept, weight, F32(0.0))
                    place = pl.ds((q * 4 + side * 2 + yh_) * W, W)
                    value = jnp.concatenate(
                        [stage[lag, 0, :, pl.ds(col, W)] * coef, -(stage[lag, 1, :, pl.ds(col, W)] * coef)], axis=0
                    )
                    high, low = halves(value)
                    rhs[pl.ds(base, W), place] = high
                    rhs[pl.ds(low_base, W), place] = low

    def load_left(c):
        for lag in range(LAGS):
            high, low = halves(own_hist[c] if lag == 0 else gat[lag, c])
            gx[:W, lag * W:(lag + 1) * W] = high
            gx[W:, lag * W:(lag + 1) * W] = low

    def multiply(q, c):
        cols = pl.ds(q * 512, 512)
        both = jnp.dot(gx[...], rhs[:LAGS * W, cols], preferred_element_type=F32)
        more = jnp.dot(gx[:W], rhs[LAGS * W:, cols], preferred_element_type=F32)
        total = both[:W] + both[W:] + more
        for yh_ in range(2):
            own[c, q, yh_] = total[:, yh_ * W:(yh_ + 1) * W]
            oth[c, q, yh_] = total[:, (2 + yh_) * W:(3 + yh_) * W]
        go(functools.partial(to_partner, q), c)

    def run(name, c):
        def when(cond):
            return pl.when(inside(c) & cond)

        if name == "S1":

            @when((t <= 14) & (t != 7))
            def _():
                go(send_own_up, c)

            @when(t == 7)
            def _():
                go(functools.partial(relay_via, 1), c)

        if name == "D7":

            @when(t <= 10)
            def _():
                go(send_own_far, c)

            @when((t == 1) | (t == 2))
            def _():
                go(send_own_seven, c)

        if name in ("P1", "P2"):
            lag = int(name[1])

            @when(t == 15)
            def _():
                relay_via(lag, c).wait_recv()
                go(functools.partial(pass_via, lag), c)

        if name in ("R2", "R3", "R4"):
            take_and_relay(int(name[1]) - 1, int(name[1]), c)
        if name in ("R5", "R6"):
            take_and_relay(int(name[1]) + 1, int(name[1]), c)
        if name == "W":
            take_and_relay(4, None, c)
            take_and_relay(5, None, c)

            @pl.when(inside(c))
            def _():
                load_left(c)

        if name == "KA":

            @pl.when(inside(c))
            def _():
                add_partner(0, 1, c)
                for way in range(2):
                    go(functools.partial(a_copy, way), c)

        if name == "KB":

            @pl.when(inside(c))
            def _():
                add_partner(1, 2, c)
                for way in range(2):
                    go(functools.partial(b_copy, way), c)

        if name == "K0":

            @pl.when(inside(c))
            def _():
                add_partner(3, 1, c)

        if name == "C":

            @pl.when(inside(c))
            def _():
                remote(a_in.at[c], a_in.at[c], a_send.at[0, 0], a_recv.at[c], left).wait_recv()
                for way in range(2):
                    own[c, 1 + way, way] = own[c, 1 + way, way] + a_in[c, way]
                    go(functools.partial(c_copy, way), c)

        if name == "X":

            @pl.when(inside(c))
            def _():
                remote(bc_in.at[c], bc_in.at[c], b_send.at[0, 0], bc_recv.at[c], left).wait_recv()
                own[c, 3, 0] = own[c, 3, 0] + (bc_in[c, 2] + bc_in[c, 1])
                own[c, 3, 1] = own[c, 3, 1] + (bc_in[c, 0] + bc_in[c, 3])
                go(y_copy, c)

        if name == "F":

            @pl.when(inside(c))
            def _():
                y_copy(c).wait_recv()
                total = own[c, 3, yh] + y_in[c]
                out_ref[:, pl.ds(pl.multiple_of(c * W, W), W)] = total.T

    first = min(AT.values()) // 4
    last = CH + max(AT.values()) // 4

    def step(s, carry):
        for slot in range(4):
            for name in PLAN:
                if AT[name] % 4 == slot:
                    run(name, s - AT[name] // 4)

            @pl.when(inside(s))
            def _():
                multiply(slot, s)

            lag = (s + 4) * 4 + slot

            @pl.when((lag >= 0) & (lag < LAGS))
            def _():
                prepare(lag)

        return carry

    lax.fori_loop(first, last + 1, step, 0)

    for c in (CH - 2, CH - 1):
        ends = [
            ((t <= 14) & (t != 7), send_own_up), (t == 7, functools.partial(relay_via, 1)),
            (t == 7, functools.partial(relay_via, 2)), (t <= 10, send_own_far),
            ((t == 1) | (t == 2), send_own_seven),
            (t == 15, functools.partial(pass_via, 1)), (t == 15, functools.partial(pass_via, 2)),
        ] + [(relays(lag), functools.partial(relay, lag)) for lag in range(2, 7)]
        for there, make in ends:

            @pl.when(there)
            def _():
                make(c).wait_send()

        for q in range(4):
            to_partner(q, c).wait_send()
        for way in range(2):
            for make in (a_copy, b_copy, c_copy):
                make(way, c).wait_send()
        y_copy(c).wait_send()


def local(self_energy, history, memory, startup_cut, weight_index, weight_table):
    smem = pl.BlockSpec(memory_space=pltpu.SMEM)
    vmem = pl.BlockSpec(memory_space=pltpu.VMEM)
    dma = pltpu.SemaphoreType.DMA
    piece = (W, W)
    out = pl.pallas_call(
        kernel,
        out_shape=jax.ShapeDtypeStruct((W, CH * W), F32),
        in_specs=[smem, smem, smem, smem, vmem, pl.BlockSpec(memory_space=pl.ANY)],
        out_specs=vmem,
        scratch_shapes=[
            pltpu.VMEM((LAGS, 2, 64, 2048), F32),
            pltpu.VMEM((2 * LAGS * W, 2048), BF16),
            pltpu.VMEM((CH, *piece), F32),
            pltpu.VMEM((LAGS, CH, *piece), F32),
            pltpu.VMEM((2, CH, *piece), F32),
            pltpu.VMEM((2 * W, LAGS * W), BF16),
            pltpu.VMEM((CH, 4, 2, *piece), F32),
            pltpu.VMEM((CH, 4, 2, *piece), F32),
            pltpu.VMEM((CH, 4, 2, *piece), F32),
            pltpu.VMEM((CH, 2, *piece), F32),
            pltpu.VMEM((CH, 4, *piece), F32),
            pltpu.VMEM((CH, *piece), F32),
            dma((LAGS,)),
            dma((LAGS, 2)), dma((LAGS, CH)), dma((2, CH)),
            dma((4, 2)), dma((3, CH)),
            dma((2, 2)), dma((CH,)),
            dma((2, 2)), dma((2, 2)), dma((CH,)),
            dma((2,)), dma((CH,)),
        ],
        compiler_params=pltpu.CompilerParams(
            collective_id=0, has_side_effects=True, vmem_limit_bytes=60 * 1024 * 1024
        ),
        name="collision",
    )(memory, startup_cut, weight_index, weight_table, history.reshape(2 * 64, 1024), self_energy)
    return out[None]


def solution(mesh):
    in_specs = (
        P("tm", None, None, "orb", None),
        P("tm", None, "orb", None),
        P(),
        P("tm"),
        P("tm", None),
        P(),
    )
    out_specs = P("tm", "orb", None)
    return jax.shard_map(local, mesh=mesh, in_specs=in_specs, out_specs=out_specs, check_vma=False)
```

time: 101 us -> 91 us (0.901)
  Pallas kernels: 97.8 us -> 87.2 us
    pallas_call x1, Pallas kernels: 97.8 us -> 87.2 us  [local(): pl.pallas_call(kernel, out_shape=jax.ShapeDtypeStruct((W, CH * W), F32),...]
where the time goes in v4:
time: 91 us; the launch traced here: 90.4 us
  Pallas kernels  87.2 us (96%)
  local copies, waits for them, and re-layouts  1.89 us (2%)
  between operations  1.3 us (1%)
    pallas_call x1, Pallas kernels, local(): pl.pallas_call(kernel, out_shape=jax.ShapeDtypeStruct((W, CH * W), F32),...  87.2 us
    unnamed x1, local copies, waits for them, and re-layouts  1.89 us

profile of v4, /device:TPU:8, one launch (start us, length us, event | category | flops | bytes accessed | tf_op | source)
XLA Modules:
  0.0 90.4 jit_solution(15367105718494797438)
XLA Ops:
  1.3 87.2 %collision.1 = f32[128,1024]{1,0:T(8,128)} custom-call(s32[1]{0:T(128)S(6)} %copy.8.mem_ref, s32[1]{0:T(128)S(6)} %copy.9.cut_ref, s32[1,8]{1,0:T(1,128)} %index_ref.1, f32[16]{0:T(128)} %table_ref.1, f32[128,1024]{1,0:T(8,128)} %bitcast.3, f32[1,2,8,64,2048]{4,3,2,1,0:T(8,128)} %se_ref.1), custom_call_target="tpu_custom_call" | custom-call | tf_op jit(solution)/shard_map/collision/pallas_call | solution.py:344
  88.6 1.9 %copy.10 = f32[1,128,1024]{2,1,0:T(8,128)} copy(f32[1,128,1024]{2,1,0:T(8,128)} %bitcast.2) | data formatting | bytes 1048576
